TPU v7x, 32 devices: a whole 2x2x4 slice. The times are simulated.
32 devices in a mesh: pp: 4 (over y, core), cp: 4 (over z), tp: 2 (over x).
Axes of the slice: x: 2, y: 2, z: 4, core: 2. Of those that a mesh axis runs over, the one named last changes fastest.
Arguments:
- queries: bfloat16 [4, 1024, 8192], P('pp', 'cp', 'tp'), may hold values from -150 to 150
- keys: bfloat16 [4, 1024, 1024], P('pp', 'cp', 'tp'), may hold values from -6 to 6
- values: bfloat16 [4, 1024, 1024], P('pp', 'cp', 'tp'), may hold values from -6 to 6
- span_order: int32 [8], replicated, may hold values from 0 to 7, each once
Outputs:
- forwarded: bfloat16 [4, 1024, 8192], P('pp', ('cp', 'tp'))
All inputs are finite; a program needn't handle non-finite values.
Results may differ from a plain program's by a relative error of at most 0.005.
Values may be sent and summed in bfloat16 or wider, within the bound.
A program may use at most 64 MiB of HBM per device.

v0:
```python
import math
import jax
import jax.numpy as jnp
from jax import lax
from jax.sharding import PartitionSpec as P

HD = 128
SPAN = 128


def passed_along(value, axis, steps):
    count = lax.axis_size(axis)
    pairs = [(source, (source + steps) % count) for source in range(count)]
    return lax.ppermute(value, axis, pairs)


def row_positions(span_order, start, count, span):
    rows = start + jnp.arange(count, dtype=jnp.int32)
    which = rows // span
    table = jnp.arange(span_order.shape[0], dtype=jnp.int32)
    picked = jnp.sum(jnp.where(which[:, None] == table[None, :], span_order[None, :], 0), axis=1)
    return picked * span + rows % span


def attend_block(carry, grouped, key_rows, value_rows, query_pos, key_pos):
    running, total, summed = carry
    score = jnp.einsum("qngd,knd->ngqk", grouped, key_rows, preferred_element_type=jnp.float32)
    score = score * (1.0 / HD**0.5)
    visible = (key_pos[None, :] <= query_pos[:, None])[None, None]
    score = jnp.where(visible, score, jnp.float32(-1e30))
    renewed = jnp.maximum(running, jnp.max(score, axis=-1))
    weight = jnp.where(visible, jnp.exp(score - renewed[..., None]), jnp.float32(0.0))
    fade = jnp.exp(running - renewed)
    total = total * fade + jnp.sum(weight, axis=-1)
    mixed = jnp.einsum(
        "ngqk,knd->ngqd",
        weight.astype(jnp.bfloat16),
        value_rows,
        preferred_element_type=jnp.float32,
    )
    summed = summed * fade[..., None] + mixed
    return (renewed, total, summed)


def attend_rows(carry, grouped, key_part, value_part, start, query_pos, span_order, span):
    count_rows = key_part.shape[0]
    kv_heads = grouped.shape[1]
    step_rows = math.gcd(count_rows, span)

    def one_block(index, state):
        first = index * step_rows
        key_rows = lax.dynamic_slice_in_dim(key_part, first, step_rows, 0).reshape(
            step_rows, kv_heads, HD
        )
        value_rows = lax.dynamic_slice_in_dim(value_part, first, step_rows, 0).reshape(
            step_rows, kv_heads, HD
        )
        key_pos = row_positions(span_order, start + first, step_rows, span)
        return attend_block(state, grouped, key_rows, value_rows, query_pos, key_pos)

    return lax.fori_loop(0, count_rows // step_rows, one_block, carry)


def to_tokens(attended):
    return lax.all_to_all(attended, "tp", split_axis=0, concat_axis=1, tiled=True)


def to_next(attended):
    return passed_along(attended, "pp", 1)


def shards(queries, keys, values, span_order):
    query_rows = queries[0]
    key_local = keys[0]
    value_local = values[0]
    local_rows = query_rows.shape[0]
    span = SPAN
    kv_heads = key_local.shape[1] // HD
    group = query_rows.shape[1] // HD // kv_heads
    my_rank = lax.axis_index("cp")
    ranks = lax.axis_size("cp")
    grouped = query_rows.reshape(local_rows, kv_heads, group, HD)
    query_pos = row_positions(span_order, my_rank * local_rows, local_rows, span)
    start_state = (
        jnp.full((kv_heads, group, local_rows), -1e30, jnp.float32),
        jnp.zeros((kv_heads, group, local_rows), jnp.float32),
        jnp.zeros((kv_heads, group, local_rows, HD), jnp.float32),
    )

    def cycle_step(turn, state):
        carry, stacked = state
        source = (my_rank - turn) % ranks
        carry = attend_rows(
            carry, grouped, stacked[0], stacked[1], source * local_rows, query_pos, span_order, span
        )
        stacked = passed_along(stacked, "cp", 1)
        return (carry, stacked)

    stacked = jnp.stack([key_local, value_local])
    carry, stacked = lax.fori_loop(0, ranks - 1, cycle_step, (start_state, stacked))
    source = (my_rank - (ranks - 1)) % ranks
    carry = attend_rows(
        carry, grouped, stacked[0], stacked[1], source * local_rows, query_pos, span_order, span
    )
    running, total, summed = carry
    attended = (summed / total[..., None]).astype(jnp.bfloat16)
    attended = jnp.transpose(attended, (2, 0, 1, 3)).reshape(local_rows, kv_heads * group * HD)
    result = to_next(to_tokens(attended))
    return result[None]


def solution(mesh):
    in_specs = (P("pp", "cp", "tp"), P("pp", "cp", "tp"), P("pp", "cp", "tp"), P())
    out_specs = P("pp", ("cp", "tp"), None)
    return jax.shard_map(shards, mesh=mesh, in_specs=in_specs, out_specs=out_specs, check_vma=False)
```

profile of v0, /device:TPU:0, one launch (start us, length us, event | category | flops | bytes accessed | tf_op | source)
XLA Modules:
  0.0 148.4 jit_solution(13930984067491431697)
XLA Ops:
  0.8 4.1 %copy.41 = bf16[1,256,4096]{1,2,0:T(8,128)(2,1)} copy(bf16[1,256,4096]{2,1,0:T(8,128)(2,1)} %param.10) | data formatting | bytes 4194304 | tf_op args[0]
  4.9 3.0 %copy.42 = bf16[256,4,8,128]{3,0,2,1:T(8,128)(2,1)S(1)} copy(bf16[256,4,8,128]{0,3,2,1:T(8,128)(2,1)} %bitcast.103) | data formatting | bytes 4194304 | tf_op jit(solution)/shard_map/while | solution.py:100
  9.1 2.4 %broadcast_in_dim.216 = f32[4,8,256,128]{3,2,1,0:T(8,128)} broadcast(f32[]{:T(128)} %constant.334.clone.1), dimensions={} | broadcast | bytes 4194308 | tf_op jit(solution)/shard_map/broadcast_in_dim | solution.py:87
  11.5 55.1 %while.79 = (s32[]{:T(128)}, f32[4,8,256]{2,1,0:T(8,128)S(1)}, f32[4,8,256]{2,1,0:T(8,128)S(1)}, f32[4,8,256,128]{3,2,1,0:T(8,128)}, bf16[2,256,512]{1,2,0:T(8,1...) while((s32[]{:T(128)}, f32[4,8,256]{2,1,0:T(8,128)S(1)}, ...), condition=%wide.region_7.8_spmd, body=%wide.region_1.7_spmd.sunk | while | flops 552655488 | bytes 28709564 | solution.py:100
  12.6 3.0 %collective-permute-start = (bf16[2,256,512]{1,2,0:T(8,128)(2,1)S(1)}, bf16[2,256,512]{1,2,0:T(8,128)(2,1)}, u32[]{:S(2)}, u32[]{:S(2)}) collective-permute-start(bf16[2,256,512]{1,2,0:T(8,128)(2,1)S(1)} %copy.82), channel_id=1, source_target_pairs={{0,2},{2,4},{4,6},{6,0},{1,3},{3,5},{5,7},{7,1},{8,10},{10,12},{12... | collective-permute-start | bytes 1572872 | tf_op jit(solution)/shard_map/while/body/eval_jaxpr/ppermute | solution.py:14
  15.7 15.2 %while.81 = (s32[]{:T(128)}, f32[4,8,256]{2,1,0:T(8,128)S(1)}, f32[4,8,256]{2,1,0:T(8,128)S(1)}, f32[4,8,256,128]{3,2,1,0:T(8,128)}, s32[]{:T(128)}, /*index=5*/...) while((s32[]{:T(128)}, f32[4,8,256]{2,1,0:T(8,128)S(1)}, ...), condition=%wide.region_6.6_spmd, body=%wide.region_2.5_spmd.sunk | while | flops 552655488 | bytes 24514796 | solution.py:61
  16.8 1.1 fusion.62
  18.0 5.3 %multiply_add_fusion.11 = f32[4,8,256,128]{3,2,1,0:T(8,128)} fusion(f32[4,8,256,128]{3,2,1,0:T(8,128)} %get-tuple-element.1191, bf16[128,4,128,1]{0,2,3,1:T(8,128)(2,1)S(1)} %bitcast.98, f32[4,128,256,8]{2,1,3,0:T(8,128)S(1)} %get-tuple-element.1170, f32[4,8,256]{2,1,0:T(8,128)S(1)} %get-tuple-element.1173, f32[4,8,256]{2,1,0:T(8,128)S(1)} %max.22, ...), kind=kOutput, calls=%fused_computation.1.clone.1 | convolution fusion | flops 275775488 | bytes 12812288 | tf_op jit(solution)/shard_map/while/body/eval_jaxpr/while/body/eval_jaxpr/ngqk,knd->ngqd/dot_general | solution.py:35
  24.4 1.1 fusion.62
  25.6 5.3 %multiply_add_fusion.11 = f32[4,8,256,128]{3,2,1,0:T(8,128)} fusion(f32[4,8,256,128]{3,2,1,0:T(8,128)} %get-tuple-element.1191, bf16[128,4,128,1]{0,2,3,1:T(8,128)(2,1)S(1)} %bitcast.98, f32[4,128,256,8]{2,1,3,0:T(8,128)S(1)} %get-tuple-element.1170, f32[4,8,256]{2,1,0:T(8,128)S(1)} %get-tuple-element.1173, f32[4,8,256]{2,1,0:T(8,128)S(1)} %max.22, ...), kind=kOutput, calls=%fused_computation.1.clone.1 | convolution fusion | flops 275775488 | bytes 12812288 | tf_op jit(solution)/shard_map/while/body/eval_jaxpr/while/body/eval_jaxpr/ngqk,knd->ngqd/dot_general | solution.py:35
  31.9 1.6 %collective-permute-start = (bf16[2,256,512]{1,2,0:T(8,128)(2,1)S(1)}, bf16[2,256,512]{1,2,0:T(8,128)(2,1)}, u32[]{:S(2)}, u32[]{:S(2)}) collective-permute-start(bf16[2,256,512]{1,2,0:T(8,128)(2,1)S(1)} %copy.82), channel_id=1, source_target_pairs={{0,2},{2,4},{4,6},{6,0},{1,3},{3,5},{5,7},{7,1},{8,10},{10,12},{12... | collective-permute-start | bytes 1572872 | tf_op jit(solution)/shard_map/while/body/eval_jaxpr/ppermute | solution.py:14
  33.6 15.2 %while.81 = (s32[]{:T(128)}, f32[4,8,256]{2,1,0:T(8,128)S(1)}, f32[4,8,256]{2,1,0:T(8,128)S(1)}, f32[4,8,256,128]{3,2,1,0:T(8,128)}, s32[]{:T(128)}, /*index=5*/...) while((s32[]{:T(128)}, f32[4,8,256]{2,1,0:T(8,128)S(1)}, ...), condition=%wide.region_6.6_spmd, body=%wide.region_2.5_spmd.sunk | while | flops 552655488 | bytes 24514796 | solution.py:61
  34.7 1.1 fusion.62
  35.9 5.3 %multiply_add_fusion.11 = f32[4,8,256,128]{3,2,1,0:T(8,128)} fusion(f32[4,8,256,128]{3,2,1,0:T(8,128)} %get-tuple-element.1191, bf16[128,4,128,1]{0,2,3,1:T(8,128)(2,1)S(1)} %bitcast.98, f32[4,128,256,8]{2,1,3,0:T(8,128)S(1)} %get-tuple-element.1170, f32[4,8,256]{2,1,0:T(8,128)S(1)} %get-tuple-element.1173, f32[4,8,256]{2,1,0:T(8,128)S(1)} %max.22, ...), kind=kOutput, calls=%fused_computation.1.clone.1 | convolution fusion | flops 275775488 | bytes 12812288 | tf_op jit(solution)/shard_map/while/body/eval_jaxpr/while/body/eval_jaxpr/ngqk,knd->ngqd/dot_general | solution.py:35
  42.3 1.1 fusion.62
  43.4 5.3 %multiply_add_fusion.11 = f32[4,8,256,128]{3,2,1,0:T(8,128)} fusion(f32[4,8,256,128]{3,2,1,0:T(8,128)} %get-tuple-element.1191, bf16[128,4,128,1]{0,2,3,1:T(8,128)(2,1)S(1)} %bitcast.98, f32[4,128,256,8]{2,1,3,0:T(8,128)S(1)} %get-tuple-element.1170, f32[4,8,256]{2,1,0:T(8,128)S(1)} %get-tuple-element.1173, f32[4,8,256]{2,1,0:T(8,128)S(1)} %max.22, ...), kind=kOutput, calls=%fused_computation.1.clone.1 | convolution fusion | flops 275775488 | bytes 12812288 | tf_op jit(solution)/shard_map/while/body/eval_jaxpr/while/body/eval_jaxpr/ngqk,knd->ngqd/dot_general | solution.py:35
  49.8 1.6 %collective-permute-start = (bf16[2,256,512]{1,2,0:T(8,128)(2,1)S(1)}, bf16[2,256,512]{1,2,0:T(8,128)(2,1)}, u32[]{:S(2)}, u32[]{:S(2)}) collective-permute-start(bf16[2,256,512]{1,2,0:T(8,128)(2,1)S(1)} %copy.82), channel_id=1, source_target_pairs={{0,2},{2,4},{4,6},{6,0},{1,3},{3,5},{5,7},{7,1},{8,10},{10,12},{12... | collective-permute-start | bytes 1572872 | tf_op jit(solution)/shard_map/while/body/eval_jaxpr/ppermute | solution.py:14
  51.4 15.2 %while.81 = (s32[]{:T(128)}, f32[4,8,256]{2,1,0:T(8,128)S(1)}, f32[4,8,256]{2,1,0:T(8,128)S(1)}, f32[4,8,256,128]{3,2,1,0:T(8,128)}, s32[]{:T(128)}, /*index=5*/...) while((s32[]{:T(128)}, f32[4,8,256]{2,1,0:T(8,128)S(1)}, ...), condition=%wide.region_6.6_spmd, body=%wide.region_2.5_spmd.sunk | while | flops 552655488 | bytes 24514796 | solution.py:61
  52.6 1.1 fusion.62
  53.7 5.3 %multiply_add_fusion.11 = f32[4,8,256,128]{3,2,1,0:T(8,128)} fusion(f32[4,8,256,128]{3,2,1,0:T(8,128)} %get-tuple-element.1191, bf16[128,4,128,1]{0,2,3,1:T(8,128)(2,1)S(1)} %bitcast.98, f32[4,128,256,8]{2,1,3,0:T(8,128)S(1)} %get-tuple-element.1170, f32[4,8,256]{2,1,0:T(8,128)S(1)} %get-tuple-element.1173, f32[4,8,256]{2,1,0:T(8,128)S(1)} %max.22, ...), kind=kOutput, calls=%fused_computation.1.clone.1 | convolution fusion | flops 275775488 | bytes 12812288 | tf_op jit(solution)/shard_map/while/body/eval_jaxpr/while/body/eval_jaxpr/ngqk,knd->ngqd/dot_general | solution.py:35
  60.2 1.1 fusion.62
  61.3 5.3 %multiply_add_fusion.11 = f32[4,8,256,128]{3,2,1,0:T(8,128)} fusion(f32[4,8,256,128]{3,2,1,0:T(8,128)} %get-tuple-element.1191, bf16[128,4,128,1]{0,2,3,1:T(8,128)(2,1)S(1)} %bitcast.98, f32[4,128,256,8]{2,1,3,0:T(8,128)S(1)} %get-tuple-element.1170, f32[4,8,256]{2,1,0:T(8,128)S(1)} %get-tuple-element.1173, f32[4,8,256]{2,1,0:T(8,128)S(1)} %max.22, ...), kind=kOutput, calls=%fused_computation.1.clone.1 | convolution fusion | flops 275775488 | bytes 12812288 | tf_op jit(solution)/shard_map/while/body/eval_jaxpr/while/body/eval_jaxpr/ngqk,knd->ngqd/dot_general | solution.py:35
  67.7 15.2 %while.80 = (s32[]{:T(128)}, f32[4,8,256]{2,1,0:T(8,128)S(1)}, f32[4,8,256]{2,1,0:T(8,128)S(1)}, f32[4,8,256,128]{3,2,1,0:T(8,128)}, s32[]{:T(128)}, /*index=5*/...) while((s32[]{:T(128)}, f32[4,8,256]{2,1,0:T(8,128)S(1)}, ...), condition=%wide.region_12.13_spmd, body=%wide.region_8.12_spmd.sunk | while | flops 552655488 | bytes 24514796 | solution.py:61
  70.0 5.3 %multiply_add_fusion.9 = f32[4,8,256,128]{3,2,1,0:T(8,128)} fusion(f32[4,8,256,128]{3,2,1,0:T(8,128)} %get-tuple-element.1287, bf16[128,4,128,1]{0,2,3,1:T(8,128)(2,1)S(1)} %bitcast.100, f32[4,128,256,8]{2,1,3,0:T(8,128)S(1)} %get-tuple-element.1154, f32[4,8,256]{2,1,0:T(8,128)S(1)} %get-tuple-element.1157, f32[4,8,256]{2,1,0:T(8,128)S(1)} %max.21, ...), kind=kOutput, calls=%fused_computation.31.clone.1 | convolution fusion | flops 275775488 | bytes 12812288 | tf_op jit(solution)/shard_map/while/body/eval_jaxpr/ngqk,knd->ngqd/dot_general | solution.py:35
  77.6 5.3 %multiply_add_fusion.9 = f32[4,8,256,128]{3,2,1,0:T(8,128)} fusion(f32[4,8,256,128]{3,2,1,0:T(8,128)} %get-tuple-element.1287, bf16[128,4,128,1]{0,2,3,1:T(8,128)(2,1)S(1)} %bitcast.100, f32[4,128,256,8]{2,1,3,0:T(8,128)S(1)} %get-tuple-element.1154, f32[4,8,256]{2,1,0:T(8,128)S(1)} %get-tuple-element.1157, f32[4,8,256]{2,1,0:T(8,128)S(1)} %max.21, ...), kind=kOutput, calls=%fused_computation.31.clone.1 | convolution fusion | flops 275775488 | bytes 12812288 | tf_op jit(solution)/shard_map/while/body/eval_jaxpr/ngqk,knd->ngqd/dot_general | solution.py:35
  82.9 2.9 %fusion.26 = bf16[256,4,8,128]{3,0,2,1:T(8,128)(2,1)S(1)} fusion(f32[4,8,256,128]{3,2,1,0:T(8,128)} %get-tuple-element.809, f32[4,8,256]{2,1,0:T(8,128)S(1)} %get-tuple-element.810), kind=kLoop, calls=%fused_computation.59 | loop fusion | flops 2097152 | bytes 6324224 | tf_op jit(solution)/shard_map/transpose | solution.py:107
  85.8 1.4 copy.44
  87.2 2.3 %all_to_all.14 = bf16[2,128,4096]{2,1,0:T(8,128)(2,1)} reshape(bf16[256,4,8,128]{3,2,1,0:T(8,128)(2,1)S(1)} %copy.44) | data formatting | bytes 4194304 | tf_op jit(solution)/shard_map/all_to_all | solution.py:65
  89.4 28.0 %all_to_all.19 = bf16[2,128,4096]{2,1,0:T(8,128)(2,1)S(1)} all-to-all(bf16[2,128,4096]{2,1,0:T(8,128)(2,1)} %all_to_all.14), channel_id=1, replica_groups=mesh['pp'=4,'cp'=4,'tp'=2] {'tp'}, dimensions={0} | all-to-all | bytes 4194304 | tf_op jit(solution)/shard_map/all_to_all | solution.py:65
  117.5 2.4 %copy.45 = bf16[128,2,4096]{0,2,1:T(8,128)(2,1)} copy(bf16[128,2,4096]{2,0,1:T(8,128)(2,1)S(1)} %bitcast.102) | data formatting | bytes 4194304 | tf_op jit(solution)/shard_map/all_to_all | solution.py:65
  119.9 25.7 %collective-permute-done.1 = bf16[128,8192]{0,1:T(8,128)(2,1)S(1)} collective-permute-done((bf16[128,8192]{0,1:T(8,128)(2,1)}, bf16[128,8192]{0,1:T(8,128)(2,1)S(1)}, u32[]{:S(2)}, u32[]{:S(2)}) %collective-permute-start.1) | collective-permute-done | bytes 2097184 | tf_op jit(solution)/shard_map/ppermute | solution.py:14
  145.6 2.9 %copy.46 = bf16[1,128,8192]{2,1,0:T(8,128)(2,1)} copy(bf16[1,128,8192]{1,2,0:T(8,128)(2,1)S(1)} %bitcast.105) | data formatting | bytes 4194304 | tf_op jit(solution)/shard_map/broadcast_in_dim | solution.py:109
  (99 shorter events, 17.4 us)
Async XLA Ops:
  0.8 7.2 %copy-start = (bf16[1,256,512]{2,1,0:T(8,128)(2,1)S(1)}, bf16[1,256,512]{2,1,0:T(8,128)(2,1)}, u32[]{:S(2)}) copy-start(bf16[1,256,512]{2,1,0:T(8,128)(2,1)} %param.11) | copy-start | bytes 786436
  0.8 7.3 %copy-start.1 = (bf16[1,256,512]{2,1,0:T(8,128)(2,1)S(1)}, bf16[1,256,512]{2,1,0:T(8,128)(2,1)}, u32[]{:S(2)}) copy-start(bf16[1,256,512]{2,1,0:T(8,128)(2,1)} %param.12) | copy-start | bytes 786436
  8.0 3.6 %copy-start.2 = (s32[8]{0:T(128)S(1)}, s32[8]{0:T(128)}, u32[]{:S(2)}) copy-start(s32[8]{0:T(128)} %param.13) | copy-start | bytes 100
  12.6 18.3 %collective-permute-start = (bf16[2,256,512]{1,2,0:T(8,128)(2,1)S(1)}, bf16[2,256,512]{1,2,0:T(8,128)(2,1)}, u32[]{:S(2)}, u32[]{:S(2)}) collective-permute-start(bf16[2,256,512]{1,2,0:T(8,128)(2,1)S(1)} %copy.82), channel_id=1, source_target_pairs={{0,2},{2,4},{4,6},{6,0},{1,3},{3,5},{5,7},{7,1},{8,10},{10,12},{12... | collective-permute-start | bytes 1572872 | tf_op jit(solution)/shard_map/while/body/eval_jaxpr/ppermute | solution.py:14
  31.9 16.8 %collective-permute-start = (bf16[2,256,512]{1,2,0:T(8,128)(2,1)S(1)}, bf16[2,256,512]{1,2,0:T(8,128)(2,1)}, u32[]{:S(2)}, u32[]{:S(2)}) collective-permute-start(bf16[2,256,512]{1,2,0:T(8,128)(2,1)S(1)} %copy.82), channel_id=1, source_target_pairs={{0,2},{2,4},{4,6},{6,0},{1,3},{3,5},{5,7},{7,1},{8,10},{10,12},{12... | collective-permute-start | bytes 1572872 | tf_op jit(solution)/shard_map/while/body/eval_jaxpr/ppermute | solution.py:14
  49.8 16.8 %collective-permute-start = (bf16[2,256,512]{1,2,0:T(8,128)(2,1)S(1)}, bf16[2,256,512]{1,2,0:T(8,128)(2,1)}, u32[]{:S(2)}, u32[]{:S(2)}) collective-permute-start(bf16[2,256,512]{1,2,0:T(8,128)(2,1)S(1)} %copy.82), channel_id=1, source_target_pairs={{0,2},{2,4},{4,6},{6,0},{1,3},{3,5},{5,7},{7,1},{8,10},{10,12},{12... | collective-permute-start | bytes 1572872 | tf_op jit(solution)/shard_map/while/body/eval_jaxpr/ppermute | solution.py:14
  119.9 25.7 %collective-permute-start.1 = (bf16[128,8192]{0,1:T(8,128)(2,1)}, bf16[128,8192]{0,1:T(8,128)(2,1)S(1)}, u32[]{:S(2)}, u32[]{:S(2)}) collective-permute-start(bf16[128,8192]{0,1:T(8,128)(2,1)} %bitcast.104), channel_id=1, source_target_pairs={{0,8},{8,16},{16,24},{24,0},{1,9},{9,17},{17,25},{25,1},{2,10},{10... | collective-permute-start | bytes 6291464 | tf_op jit(solution)/shard_map/ppermute | solution.py:14
where the time goes:
time: 149 us; the launch traced here: 148 us
  matrix products  49.5 us (33%)
  blocking collectives  28 us (19%)
  waiting for transfers between devices  25.7 us (17%)
  local copies, waits for them, and re-layouts  23.4 us (16%)
  other arithmetic  15 us (10%)
  starting transfers between devices  6.18 us (4%)
    dot_general x8, matrix products, attend_block(): jnp.einsum('ngqk,knd->ngqd', weight.astype(jnp.bfloat16), value_rows, pre...  42.5 us
    all_to_all x1, blocking collectives, to_tokens(): lax.all_to_all(attended, 'tp', split_axis=0, concat_axis=1, tiled=True)  28 us
    ppermute x4, waiting for transfers between devices, passed_along(): return lax.ppermute(value, axis, pairs)  25.7 us
    reduce_sum x8, other arithmetic, attend_block(): total = total * fade + jnp.sum(weight, axis=-1)  8.74 us
    dot_general x8, matrix products, attend_block(): jnp.einsum('qngd,knd->ngqk', grouped, key_rows, preferred_element_type=jn...  6.99 us
    ppermute x4, starting transfers between devices, passed_along(): return lax.ppermute(value, axis, pairs)  6.18 us
    all_to_all x2, local copies, waits for them, and re-layouts, to_tokens(): lax.all_to_all(attended, 'tp', split_axis=0, concat_axis=1, tiled=True)  4.73 us
    unnamed x9, local copies, waits for them, and re-layouts  4.41 us
  transfers between devices with their start and end apart: 4, of which 1 were waited for; matrix products, arithmetic and copies ran while one was open for 31% of the time, Pallas kernels for 0%

commit v1 on v0

--- a/solution.py
+++ b/solution.py
@@ -62,7 +62,10 @@
 
 
 def to_tokens(attended):
-    return lax.all_to_all(attended, "tp", split_axis=0, concat_axis=1, tiled=True)
+    return jnp.concatenate(
+        lax.all_to_all(jnp.stack(jnp.split(attended, lax.axis_size("tp"), axis=0)), "tp", 0, 0),
+        axis=1,
+    )
 
 
 def to_next(attended):

time: 149 us -> 149 us (level)
    while x8 -> x9, local copies, waits for them, and re-layouts: 0.03 us -> 5.39 us  [the longest x1 5.37 us: attend_rows(): return lax.fori_loop(0, count_rows // step_rows, one_block, carry)]
    all_to_all x2 -> x0, local copies, waits for them, and re-layouts: 4.73 us -> none  [to_tokens(): lax.all_to_all(attended, 'tp', split_axis=0, concat_axis=1, tiled=True)]
    broadcast_in_dim x1 -> x0, local copies, waits for them, and re-layouts: 2.88 us -> none  [shards(): return result[None]]
    reshape x0 -> x1, local copies, waits for them, and re-layouts: none -> 2.88 us  [to_tokens(): jnp.concatenate(lax.all_to_all(jnp.stack(jnp.split(attended, lax.axis_siz...]
    unnamed x9 -> x10, local copies, waits for them, and re-layouts: 4.41 us -> 5.73 us
where the time goes in v1:
time: 149 us
  matrix products  49.5 us (33%)
  blocking collectives  26.8 us (18%)
  waiting for transfers between devices  25.7 us (17%)
  local copies, waits for them, and re-layouts  24.6 us (17%)
  other arithmetic  15 us (10%)
  starting transfers between devices  6.18 us (4%)
    dot_general x8, matrix products, attend_block(): jnp.einsum('ngqk,knd->ngqd', weight.astype(jnp.bfloat16), value_rows, pre...  42.5 us
    all_to_all x1, blocking collectives, to_tokens(): lax.all_to_all(jnp.stack(jnp.split(attended, lax.axis_size('tp'), axis=0)...  26.8 us
    ppermute x4, waiting for transfers between devices, passed_along(): return lax.ppermute(value, axis, pairs)  25.7 us
    reduce_sum x8, other arithmetic, attend_block(): total = total * fade + jnp.sum(weight, axis=-1)  8.74 us
    dot_general x8, matrix products, attend_block(): jnp.einsum('qngd,knd->ngqk', grouped, key_rows, preferred_element_type=jn...  6.99 us
    ppermute x4, starting transfers between devices, passed_along(): return lax.ppermute(value, axis, pairs)  6.18 us
    unnamed x10, local copies, waits for them, and re-layouts  5.73 us
    while x1, local copies, waits for them, and re-layouts, attend_rows(): return lax.fori_loop(0, count_rows // step_rows, one_block, carry)  5.37 us
  transfers between devices with their start and end apart: 4, of which 1 were waited for; matrix products, arithmetic and copies ran while one was open for 31% of the time, Pallas kernels for 0%

profile of v1, /device:TPU:0, one launch (start us, length us, event | category | flops | bytes accessed | tf_op | source)
XLA Modules:
  0.0 148.5 jit_solution(11376030599148224738)
XLA Ops:
  0.8 4.1 %copy.28 = bf16[1,256,4096]{1,2,0:T(8,128)(2,1)} copy(bf16[1,256,4096]{2,1,0:T(8,128)(2,1)} %param.10) | data formatting | bytes 4194304 | tf_op args[0]
  4.9 3.0 %copy.29 = bf16[256,4,8,128]{3,0,2,1:T(8,128)(2,1)S(1)} copy(bf16[256,4,8,128]{0,3,2,1:T(8,128)(2,1)} %bitcast.104) | data formatting | bytes 4194304 | tf_op jit(solution)/shard_map/while | solution.py:103
  9.1 2.4 %broadcast_in_dim.216 = f32[4,8,256,128]{3,2,1,0:T(8,128)} broadcast(f32[]{:T(128)} %constant.334.clone.1), dimensions={} | broadcast | bytes 4194308 | tf_op jit(solution)/shard_map/broadcast_in_dim | solution.py:90
  11.5 55.1 %while.79 = (s32[]{:T(128)}, f32[4,8,256]{2,1,0:T(8,128)S(1)}, f32[4,8,256]{2,1,0:T(8,128)S(1)}, f32[4,8,256,128]{3,2,1,0:T(8,128)}, bf16[2,256,512]{1,2,0:T(8,1...) while((s32[]{:T(128)}, f32[4,8,256]{2,1,0:T(8,128)S(1)}, ...), condition=%wide.region_7.8_spmd, body=%wide.region_1.7_spmd.sunk | while | flops 552655488 | bytes 28709564 | solution.py:103
  12.6 3.0 %collective-permute-start = (bf16[2,256,512]{1,2,0:T(8,128)(2,1)S(1)}, bf16[2,256,512]{1,2,0:T(8,128)(2,1)}, u32[]{:S(2)}, u32[]{:S(2)}) collective-permute-start(bf16[2,256,512]{1,2,0:T(8,128)(2,1)S(1)} %copy.68), channel_id=1, source_target_pairs={{0,2},{2,4},{4,6},{6,0},{1,3},{3,5},{5,7},{7,1},{8,10},{10,12},{12... | collective-permute-start | bytes 1572872 | tf_op jit(solution)/shard_map/while/body/eval_jaxpr/ppermute | solution.py:14
  15.7 15.2 %while.81 = (s32[]{:T(128)}, f32[4,8,256]{2,1,0:T(8,128)S(1)}, f32[4,8,256]{2,1,0:T(8,128)S(1)}, f32[4,8,256,128]{3,2,1,0:T(8,128)}, s32[]{:T(128)}, /*index=5*/...) while((s32[]{:T(128)}, f32[4,8,256]{2,1,0:T(8,128)S(1)}, ...), condition=%wide.region_6.6_spmd, body=%wide.region_2.5_spmd.sunk | while | flops 552655488 | bytes 24514796 | solution.py:61
  16.8 1.1 fusion.63
  18.0 5.3 %multiply_add_fusion.11 = f32[4,8,256,128]{3,2,1,0:T(8,128)} fusion(f32[4,8,256,128]{3,2,1,0:T(8,128)} %get-tuple-element.1174, bf16[128,4,128,1]{0,2,3,1:T(8,128)(2,1)S(1)} %bitcast.99, f32[4,128,256,8]{2,1,3,0:T(8,128)S(1)} %get-tuple-element.1153, f32[4,8,256]{2,1,0:T(8,128)S(1)} %get-tuple-element.1156, f32[4,8,256]{2,1,0:T(8,128)S(1)} %max.22, ...), kind=kOutput, calls=%fused_computation.1.clone.1 | convolution fusion | flops 275775488 | bytes 12812288 | tf_op jit(solution)/shard_map/while/body/eval_jaxpr/while/body/eval_jaxpr/ngqk,knd->ngqd/dot_general | solution.py:35
  24.4 1.1 fusion.63
  25.6 5.3 %multiply_add_fusion.11 = f32[4,8,256,128]{3,2,1,0:T(8,128)} fusion(f32[4,8,256,128]{3,2,1,0:T(8,128)} %get-tuple-element.1174, bf16[128,4,128,1]{0,2,3,1:T(8,128)(2,1)S(1)} %bitcast.99, f32[4,128,256,8]{2,1,3,0:T(8,128)S(1)} %get-tuple-element.1153, f32[4,8,256]{2,1,0:T(8,128)S(1)} %get-tuple-element.1156, f32[4,8,256]{2,1,0:T(8,128)S(1)} %max.22, ...), kind=kOutput, calls=%fused_computation.1.clone.1 | convolution fusion | flops 275775488 | bytes 12812288 | tf_op jit(solution)/shard_map/while/body/eval_jaxpr/while/body/eval_jaxpr/ngqk,knd->ngqd/dot_general | solution.py:35
  31.9 1.6 %collective-permute-start = (bf16[2,256,512]{1,2,0:T(8,128)(2,1)S(1)}, bf16[2,256,512]{1,2,0:T(8,128)(2,1)}, u32[]{:S(2)}, u32[]{:S(2)}) collective-permute-start(bf16[2,256,512]{1,2,0:T(8,128)(2,1)S(1)} %copy.68), channel_id=1, source_target_pairs={{0,2},{2,4},{4,6},{6,0},{1,3},{3,5},{5,7},{7,1},{8,10},{10,12},{12... | collective-permute-start | bytes 1572872 | tf_op jit(solution)/shard_map/while/body/eval_jaxpr/ppermute | solution.py:14
  33.6 15.2 %while.81 = (s32[]{:T(128)}, f32[4,8,256]{2,1,0:T(8,128)S(1)}, f32[4,8,256]{2,1,0:T(8,128)S(1)}, f32[4,8,256,128]{3,2,1,0:T(8,128)}, s32[]{:T(128)}, /*index=5*/...) while((s32[]{:T(128)}, f32[4,8,256]{2,1,0:T(8,128)S(1)}, ...), condition=%wide.region_6.6_spmd, body=%wide.region_2.5_spmd.sunk | while | flops 552655488 | bytes 24514796 | solution.py:61
  34.7 1.1 fusion.63
  35.9 5.3 %multiply_add_fusion.11 = f32[4,8,256,128]{3,2,1,0:T(8,128)} fusion(f32[4,8,256,128]{3,2,1,0:T(8,128)} %get-tuple-element.1174, bf16[128,4,128,1]{0,2,3,1:T(8,128)(2,1)S(1)} %bitcast.99, f32[4,128,256,8]{2,1,3,0:T(8,128)S(1)} %get-tuple-element.1153, f32[4,8,256]{2,1,0:T(8,128)S(1)} %get-tuple-element.1156, f32[4,8,256]{2,1,0:T(8,128)S(1)} %max.22, ...), kind=kOutput, calls=%fused_computation.1.clone.1 | convolution fusion | flops 275775488 | bytes 12812288 | tf_op jit(solution)/shard_map/while/body/eval_jaxpr/while/body/eval_jaxpr/ngqk,knd->ngqd/dot_general | solution.py:35
  42.3 1.1 fusion.63
  43.4 5.3 %multiply_add_fusion.11 = f32[4,8,256,128]{3,2,1,0:T(8,128)} fusion(f32[4,8,256,128]{3,2,1,0:T(8,128)} %get-tuple-element.1174, bf16[128,4,128,1]{0,2,3,1:T(8,128)(2,1)S(1)} %bitcast.99, f32[4,128,256,8]{2,1,3,0:T(8,128)S(1)} %get-tuple-element.1153, f32[4,8,256]{2,1,0:T(8,128)S(1)} %get-tuple-element.1156, f32[4,8,256]{2,1,0:T(8,128)S(1)} %max.22, ...), kind=kOutput, calls=%fused_computation.1.clone.1 | convolution fusion | flops 275775488 | bytes 12812288 | tf_op jit(solution)/shard_map/while/body/eval_jaxpr/while/body/eval_jaxpr/ngqk,knd->ngqd/dot_general | solution.py:35
  49.8 1.6 %collective-permute-start = (bf16[2,256,512]{1,2,0:T(8,128)(2,1)S(1)}, bf16[2,256,512]{1,2,0:T(8,128)(2,1)}, u32[]{:S(2)}, u32[]{:S(2)}) collective-permute-start(bf16[2,256,512]{1,2,0:T(8,128)(2,1)S(1)} %copy.68), channel_id=1, source_target_pairs={{0,2},{2,4},{4,6},{6,0},{1,3},{3,5},{5,7},{7,1},{8,10},{10,12},{12... | collective-permute-start | bytes 1572872 | tf_op jit(solution)/shard_map/while/body/eval_jaxpr/ppermute | solution.py:14
  51.4 15.2 %while.81 = (s32[]{:T(128)}, f32[4,8,256]{2,1,0:T(8,128)S(1)}, f32[4,8,256]{2,1,0:T(8,128)S(1)}, f32[4,8,256,128]{3,2,1,0:T(8,128)}, s32[]{:T(128)}, /*index=5*/...) while((s32[]{:T(128)}, f32[4,8,256]{2,1,0:T(8,128)S(1)}, ...), condition=%wide.region_6.6_spmd, body=%wide.region_2.5_spmd.sunk | while | flops 552655488 | bytes 24514796 | solution.py:61
  52.6 1.1 fusion.63
  53.7 5.3 %multiply_add_fusion.11 = f32[4,8,256,128]{3,2,1,0:T(8,128)} fusion(f32[4,8,256,128]{3,2,1,0:T(8,128)} %get-tuple-element.1174, bf16[128,4,128,1]{0,2,3,1:T(8,128)(2,1)S(1)} %bitcast.99, f32[4,128,256,8]{2,1,3,0:T(8,128)S(1)} %get-tuple-element.1153, f32[4,8,256]{2,1,0:T(8,128)S(1)} %get-tuple-element.1156, f32[4,8,256]{2,1,0:T(8,128)S(1)} %max.22, ...), kind=kOutput, calls=%fused_computation.1.clone.1 | convolution fusion | flops 275775488 | bytes 12812288 | tf_op jit(solution)/shard_map/while/body/eval_jaxpr/while/body/eval_jaxpr/ngqk,knd->ngqd/dot_general | solution.py:35
  60.2 1.1 fusion.63
  61.3 5.3 %multiply_add_fusion.11 = f32[4,8,256,128]{3,2,1,0:T(8,128)} fusion(f32[4,8,256,128]{3,2,1,0:T(8,128)} %get-tuple-element.1174, bf16[128,4,128,1]{0,2,3,1:T(8,128)(2,1)S(1)} %bitcast.99, f32[4,128,256,8]{2,1,3,0:T(8,128)S(1)} %get-tuple-element.1153, f32[4,8,256]{2,1,0:T(8,128)S(1)} %get-tuple-element.1156, f32[4,8,256]{2,1,0:T(8,128)S(1)} %max.22, ...), kind=kOutput, calls=%fused_computation.1.clone.1 | convolution fusion | flops 275775488 | bytes 12812288 | tf_op jit(solution)/shard_map/while/body/eval_jaxpr/while/body/eval_jaxpr/ngqk,knd->ngqd/dot_general | solution.py:35
  67.7 15.2 %while.80 = (s32[]{:T(128)}, f32[4,8,256]{2,1,0:T(8,128)S(1)}, f32[4,8,256]{2,1,0:T(8,128)S(1)}, f32[4,8,256,128]{3,2,1,0:T(8,128)}, s32[]{:T(128)}, /*index=5*/...) while((s32[]{:T(128)}, f32[4,8,256]{2,1,0:T(8,128)S(1)}, ...), condition=%wide.region_12.13_spmd, body=%wide.region_8.12_spmd.sunk | while | flops 552655488 | bytes 24514796 | solution.py:61
  68.9 1.1 fusion.56
  70.0 5.3 %multiply_add_fusion.9 = f32[4,8,256,128]{3,2,1,0:T(8,128)} fusion(f32[4,8,256,128]{3,2,1,0:T(8,128)} %get-tuple-element.1270, bf16[128,4,128,1]{0,2,3,1:T(8,128)(2,1)S(1)} %bitcast.101, f32[4,128,256,8]{2,1,3,0:T(8,128)S(1)} %get-tuple-element.1137, f32[4,8,256]{2,1,0:T(8,128)S(1)} %get-tuple-element.1140, f32[4,8,256]{2,1,0:T(8,128)S(1)} %max.21, ...), kind=kOutput, calls=%fused_computation.31.clone.1 | convolution fusion | flops 275775488 | bytes 12812288 | tf_op jit(solution)/shard_map/while/body/eval_jaxpr/ngqk,knd->ngqd/dot_general | solution.py:35
  77.6 5.3 %multiply_add_fusion.9 = f32[4,8,256,128]{3,2,1,0:T(8,128)} fusion(f32[4,8,256,128]{3,2,1,0:T(8,128)} %get-tuple-element.1270, bf16[128,4,128,1]{0,2,3,1:T(8,128)(2,1)S(1)} %bitcast.101, f32[4,128,256,8]{2,1,3,0:T(8,128)S(1)} %get-tuple-element.1137, f32[4,8,256]{2,1,0:T(8,128)S(1)} %get-tuple-element.1140, f32[4,8,256]{2,1,0:T(8,128)S(1)} %max.21, ...), kind=kOutput, calls=%fused_computation.31.clone.1 | convolution fusion | flops 275775488 | bytes 12812288 | tf_op jit(solution)/shard_map/while/body/eval_jaxpr/ngqk,knd->ngqd/dot_general | solution.py:35
  82.9 5.4 %copy.31 = f32[4,8,256,128]{2,3,1,0:T(8,128)} copy(f32[4,8,256,128]{3,2,1,0:T(8,128)} %get-tuple-element.809) | data formatting | bytes 8388608 | tf_op jit(solution)/shard_map/while | solution.py:61
  88.3 2.7 %fusion.26 = bf16[256,4,8,128]{0,3,2,1:T(8,128)(2,1)S(1)} fusion(f32[4,8,256,128]{2,3,1,0:T(8,128)} %copy.31, f32[4,8,256]{2,1,0:T(8,128)S(1)} %get-tuple-element.810), kind=kLoop, calls=%fused_computation.60 | loop fusion | flops 2097152 | bytes 6324224 | tf_op jit(solution)/shard_map/transpose | solution.py:110
  91.8 26.8 %all_to_all.5 = bf16[2,128,4096]{1,2,0:T(8,128)(2,1)S(1)} all-to-all(bf16[2,128,4096]{1,2,0:T(8,128)(2,1)S(1)} %pad_maximum_fusion), channel_id=1, replica_groups=mesh['pp'=4,'cp'=4,'tp'=2] {'tp'}, dimensions={0} | all-to-all | bytes 4194304 | tf_op jit(solution)/shard_map/all_to_all | solution.py:66
  118.6 2.9 %copy.32 = bf16[128,8192]{1,0:T(8,128)(2,1)} copy(bf16[128,8192]{0,1:T(8,128)(2,1)S(1)} %bitcast.103) | data formatting | bytes 4194304 | tf_op jit(solution)/shard_map/reshape | solution.py:65
  121.5 25.7 %collective-permute-done.1 = bf16[128,8192]{1,0:T(8,128)(2,1)S(1)} collective-permute-done((bf16[128,8192]{1,0:T(8,128)(2,1)}, bf16[128,8192]{1,0:T(8,128)(2,1)S(1)}, u32[]{:S(2)}, u32[]{:S(2)}) %collective-permute-start.1) | collective-permute-done | bytes 2097184 | tf_op jit(solution)/shard_map/ppermute | solution.py:14
  147.2 1.3 copy.89
  (100 shorter events, 17.1 us)
Async XLA Ops:
  0.8 7.2 %copy-start = (bf16[1,256,512]{2,1,0:T(8,128)(2,1)S(1)}, bf16[1,256,512]{2,1,0:T(8,128)(2,1)}, u32[]{:S(2)}) copy-start(bf16[1,256,512]{2,1,0:T(8,128)(2,1)} %param.11) | copy-start | bytes 786436
  0.8 7.3 %copy-start.1 = (bf16[1,256,512]{2,1,0:T(8,128)(2,1)S(1)}, bf16[1,256,512]{2,1,0:T(8,128)(2,1)}, u32[]{:S(2)}) copy-start(bf16[1,256,512]{2,1,0:T(8,128)(2,1)} %param.12) | copy-start | bytes 786436
  8.0 3.6 %copy-start.2 = (s32[8]{0:T(128)S(1)}, s32[8]{0:T(128)}, u32[]{:S(2)}) copy-start(s32[8]{0:T(128)} %param.13) | copy-start | bytes 100
  12.6 18.3 %collective-permute-start = (bf16[2,256,512]{1,2,0:T(8,128)(2,1)S(1)}, bf16[2,256,512]{1,2,0:T(8,128)(2,1)}, u32[]{:S(2)}, u32[]{:S(2)}) collective-permute-start(bf16[2,256,512]{1,2,0:T(8,128)(2,1)S(1)} %copy.68), channel_id=1, source_target_pairs={{0,2},{2,4},{4,6},{6,0},{1,3},{3,5},{5,7},{7,1},{8,10},{10,12},{12... | collective-permute-start | bytes 1572872 | tf_op jit(solution)/shard_map/while/body/eval_jaxpr/ppermute | solution.py:14
  31.9 16.8 %collective-permute-start = (bf16[2,256,512]{1,2,0:T(8,128)(2,1)S(1)}, bf16[2,256,512]{1,2,0:T(8,128)(2,1)}, u32[]{:S(2)}, u32[]{:S(2)}) collective-permute-start(bf16[2,256,512]{1,2,0:T(8,128)(2,1)S(1)} %copy.68), channel_id=1, source_target_pairs={{0,2},{2,4},{4,6},{6,0},{1,3},{3,5},{5,7},{7,1},{8,10},{10,12},{12... | collective-permute-start | bytes 1572872 | tf_op jit(solution)/shard_map/while/body/eval_jaxpr/ppermute | solution.py:14
  49.8 16.8 %collective-permute-start = (bf16[2,256,512]{1,2,0:T(8,128)(2,1)S(1)}, bf16[2,256,512]{1,2,0:T(8,128)(2,1)}, u32[]{:S(2)}, u32[]{:S(2)}) collective-permute-start(bf16[2,256,512]{1,2,0:T(8,128)(2,1)S(1)} %copy.68), channel_id=1, source_target_pairs={{0,2},{2,4},{4,6},{6,0},{1,3},{3,5},{5,7},{7,1},{8,10},{10,12},{12... | collective-permute-start | bytes 1572872 | tf_op jit(solution)/shard_map/while/body/eval_jaxpr/ppermute | solution.py:14
  121.5 25.7 %collective-permute-start.1 = (bf16[128,8192]{1,0:T(8,128)(2,1)}, bf16[128,8192]{1,0:T(8,128)(2,1)S(1)}, u32[]{:S(2)}, u32[]{:S(2)}) collective-permute-start(bf16[128,8192]{1,0:T(8,128)(2,1)} %copy.32), channel_id=1, source_target_pairs={{0,8},{8,16},{16,24},{24,0},{1,9},{9,17},{17,25},{25,1},{2,10},{10... | collective-permute-start | bytes 6291464 | tf_op jit(solution)/shard_map/ppermute | solution.py:14
